TPU v7x, 32 devices: a whole 2x2x4 slice. The times are simulated.
32 devices in a mesh: space: 8 (over z, y), chan: 2 (over core), filt: 2 (over x).
Axes of the slice: x: 2, y: 2, z: 4, core: 2. Of those that a mesh axis runs over, the one named last changes fastest.
Arguments:
- activation: bfloat16 [8, 512, 512], P('space', ('chan', 'filt')), may hold values from -6 to 6
- kernel: bfloat16 [3, 3, 3, 512, 512], P(None, None, None, 'filt', 'chan'), may hold values from -0.0546875 to 0.0546875
- out_grad: bfloat16 [8, 512, 512], P('space', 'filt', 'chan'), may hold values from -6 to 6
Outputs:
- output: bfloat16 [8, 512, 512], P('space', 'filt', 'chan')
- input_grad: bfloat16 [8, 512, 512], P('space', ('chan', 'filt'))
- kernel_grad: float32 [3, 3, 3, 512, 512], P(None, None, None, 'filt', 'chan')
All inputs are finite; a program needn't handle non-finite values.
Results may differ from a plain program's by a relative error of at most 0.001.
Values may be sent and summed in bfloat16 or wider, within the bound.
A program may use at most 128 MiB of HBM per device.

v0:
```python
import jax
import jax.numpy as jnp
from jax import lax
from jax.sharding import PartitionSpec as P

W = 16


def padded(x, sides, width):
    for axis, dim in sides:
        size, length = (lax.axis_size(axis), x.shape[dim])
        up = [(i, (i + 1) % size) for i in range(size - 1)]
        down = [(j, i) for i, j in up]
        last = lax.slice_in_dim(x, length - width, length, axis=dim)
        first = lax.slice_in_dim(x, 0, width, axis=dim)
        before = lax.ppermute(last, axis, up)
        after = lax.ppermute(first, axis, down)
        x = jnp.concatenate([before, x, after], axis=dim)
    return x


def plane_window(widened, plane, row_step, col_step, masks):
    begin = row_step * W + col_step
    return widened[:, :, begin : begin + plane] * masks[col_step]


def body(activation, kernel, out_grad):
    depth = activation.shape[0]
    plane = activation.shape[2]
    panels = lax.all_gather(activation, "filt", axis=1, tiled=True)
    rimmed = padded(panels, (("space", 0),), 1)
    grad_full = lax.all_gather(out_grad, "chan", axis=2, tiled=True)
    grad_rimmed = padded(grad_full, (("space", 0),), 1)
    column = lax.iota(jnp.int32, plane) % W
    masks = [
        ((column + step - 1 >= 0) & (column + step - 1 < W)).astype(jnp.bfloat16)
        for step in range(3)
    ]
    chan_local = rimmed.shape[1]
    filt_local = grad_rimmed.shape[1]
    wide_input = jnp.pad(rimmed, ((0, 0), (0, 0), (W + 1, W + 1)))
    wide_grad = jnp.pad(grad_rimmed, ((0, 0), (0, 0), (W + 1, W + 1)))
    forward = jnp.zeros((depth, filt_local, plane), jnp.float32)
    backward = jnp.zeros((depth, chan_local, plane), jnp.float32)
    taps = []
    for a in range(3):
        input_slab = wide_input[a : a + depth]
        grad_slab = wide_grad[2 - a : 2 - a + depth]
        for b in range(3):
            window = jnp.concatenate(
                [plane_window(input_slab, plane, b, c, masks) for c in range(3)], axis=1
            )
            grad_window = jnp.concatenate(
                [plane_window(grad_slab, plane, 2 - b, 2 - c, masks) for c in range(3)], axis=1
            )
            weights = kernel[a, b]
            forward_weights = weights.transpose(1, 0, 2).reshape(filt_local, 3 * chan_local)
            backward_weights = weights.reshape(3 * filt_local, chan_local)
            forward = forward + jnp.einsum(
                "fk,zkp->zfp", forward_weights, window, preferred_element_type=jnp.float32
            )
            backward = backward + jnp.einsum(
                "fk,zfp->zkp", backward_weights, grad_window, preferred_element_type=jnp.float32
            )
            joined = jnp.einsum(
                "zfp,zkp->fk", grad_full, window, preferred_element_type=jnp.float32
            )
            taps.append(joined.reshape(filt_local, 3, chan_local).transpose(1, 0, 2))
    output = lax.psum_scatter(forward, "chan", scatter_dimension=2, tiled=True).astype(jnp.bfloat16)
    input_grad = lax.psum_scatter(backward, "filt", scatter_dimension=1, tiled=True).astype(
        jnp.bfloat16
    )
    local_grad = jnp.stack(taps).reshape(3, 3, 3, filt_local, chan_local)
    total = lax.psum(local_grad, "space")
    cells = depth * lax.axis_size("space") * plane
    kernel_grad = total / jnp.sqrt(jnp.float32(cells))
    return (output, input_grad, kernel_grad)


def solution(mesh):
    placed = (
        P("space", ("chan", "filt"), None),
        P(None, None, None, "filt", "chan"),
        P("space", "filt", "chan"),
    )
    return jax.shard_map(
        body,
        mesh=mesh,
        in_specs=placed,
        out_specs=(
            P("space", "filt", "chan"),
            P("space", ("chan", "filt"), None),
            P(None, None, None, "filt", "chan"),
        ),
        check_vma=False,
    )
```

profile of v0, /device:TPU:0, one launch (start us, length us, event | category | flops | bytes accessed | tf_op | source)
XLA Modules:
  0.0 349.9 jit_solution(17022431209506651574)
XLA Ops:
  8.0 7.4 %all_gather.6 = bf16[1,256,512]{2,1,0:T(8,128)(2,1)S(1)} all-gather(bf16[1,128,512]{2,1,0:T(8,128)(2,1)} %param.3), channel_id=1, replica_groups=mesh['space'=8,'chan'=2,'filt'=2] {'filt'}, dimensions={1}, use_global_device_ids=true | all-gather | bytes 393216 | tf_op jit(solution)/shard_map/all_gather | solution.py:30
  15.4 1.3 collective-permute-start.1
  16.7 5.3 %collective-permute-start = (bf16[1,256,512]{2,1,0:T(8,128)(2,1)S(1)}, bf16[1,256,512]{2,1,0:T(8,128)(2,1)}, u32[]{:S(2)}, u32[]{:S(2)}) collective-permute-start(bf16[1,256,512]{2,1,0:T(8,128)(2,1)S(1)} %all_gather.6), channel_id=1, source_target_pairs={{0,4},{4,8},{8,12},{12,16},{16,20},{20,24},{24,28},{1,5},{5,9},{9,... | collective-permute-start | bytes 786440 | tf_op jit(solution)/shard_map/ppermute | solution.py:16
  22.0 2.3 all_gather.7
  24.2 4.5 %collective-permute-start.2 = (bf16[1,256,512]{2,1,0:T(8,128)(2,1)S(1)}, bf16[1,256,512]{2,1,0:T(8,128)(2,1)}, u32[]{:S(2)}, u32[]{:S(2)}) collective-permute-start(bf16[1,256,512]{2,1,0:T(8,128)(2,1)S(1)} %all_gather.7), channel_id=1, source_target_pairs={{0,4},{4,8},{8,12},{12,16},{16,20},{20,24},{24,28},{1,5},{5,9},{9,... | collective-permute-start | bytes 786440 | tf_op jit(solution)/shard_map/ppermute | solution.py:16
  28.8 1.3 collective-permute-start.3
  30.1 3.2 fusion.87
  33.3 2.3 copy.42
  35.6 1.9 copy.43
  44.1 1.5 select_maximum_fusion.2
  46.3 1.6 select_maximum_fusion
  48.0 1.9 slice_multiply_fusion
  49.8 2.8 slice_multiply_fusion.26
  53.0 4.0 %slice_multiply_fusion.2 = (bf16[1,256,512]{2,1,0:T(8,128)(2,1)}, bf16[1,256,512]{2,1,0:T(8,128)(2,1)}, bf16[1,256,512]{2,1,0:T(8,128)(2,1)}, bf16[1,256,512]{2,...) fusion(bf16[3,256,546]{2,1,0:T(8,128)(2,1)S(1)} %select_maximum, ...), kind=kLoop, calls=%fused_computation.112 | loop fusion | flops 2228224 | bytes 8914944 | tf_op jit(solution)/shard_map/mul | solution.py:24
  64.6 1.8 broadcast_multiply_fusion.3
  66.4 1.3 pad_maximum_fusion.6
  70.1 1.6 fusion.13
  88.0 1.3 fusion.5
  89.3 1.3 fusion.4
  90.5 1.3 fusion.3
  91.8 1.3 fusion.2
  94.4 8.1 %copy.39 = f32[3,3,3,256,256]{4,3,2,1,0:T(8,128)} copy(f32[3,3,3,256,256]{3,4,2,1,0:T(8,128)} %bitcast.227) | data formatting | bytes 14155776 | tf_op jit(solution)/shard_map/reshape | solution.py:73
  106.0 229.8 %all-reduce.4.cloned.1.call-done = f32[3,3,3,256,256]{4,3,2,1,0:T(8,128)} async-done(((f32[3,3,3,256,256]{4,3,2,1,0:T(8,128)}), f32[3,3,3,256,256]{4,3,2,1,0:T(8,128)}) %all-reduce.4.cloned.1.call-update) | async-done | bytes 7077904 | tf_op jit(solution)/shard_map/psum | solution.py:74
  335.8 6.7 %broadcast_multiply_fusion = f32[3,3,3,256,256]{4,3,2,1,0:T(8,128)} fusion(f32[3,3,3,256,256]{4,3,2,1,0:T(8,128)} %all-reduce.4.cloned.1.call-done), kind=kLoop, calls=%fused_computation | loop fusion | flops 1769472 | bytes 14155776 | tf_op jit(solution)/shard_map/div | solution.py:76
  (173 shorter events, 38.4 us)
Async XLA Ops:
  8.0 94.5 %reduce-scatter.3.cloned.1.call-start = ((), (), s32[]{:S(2)}) async-start(), calls=%async_computation.2 | async-start | bytes 786432 | tf_op jit(solution)/shard_map/reduce_scatter | solution.py:69
  15.4 28.7 %collective-permute-start.1 = (bf16[1,256,512]{2,1,0:T(8,128)(2,1)S(1)}, bf16[1,256,512]{2,1,0:T(8,128)(2,1)}, u32[]{:S(2)}, u32[]{:S(2)}) collective-permute-start(bf16[1,256,512]{2,1,0:T(8,128)(2,1)S(1)} %all_gather.6), channel_id=1, source_target_pairs={{4,0},{8,4},{12,8},{16,12},{20,16},{24,20},{28,24},{5,1},{9,5},{13... | collective-permute-start | bytes 786440 | tf_op jit(solution)/shard_map/ppermute | solution.py:17
  16.7 27.4 %collective-permute-start = (bf16[1,256,512]{2,1,0:T(8,128)(2,1)S(1)}, bf16[1,256,512]{2,1,0:T(8,128)(2,1)}, u32[]{:S(2)}, u32[]{:S(2)}) collective-permute-start(bf16[1,256,512]{2,1,0:T(8,128)(2,1)S(1)} %all_gather.6), channel_id=1, source_target_pairs={{0,4},{4,8},{8,12},{12,16},{16,20},{20,24},{24,28},{1,5},{5,9},{9,... | collective-permute-start | bytes 786440 | tf_op jit(solution)/shard_map/ppermute | solution.py:16
  24.2 22.1 %collective-permute-start.2 = (bf16[1,256,512]{2,1,0:T(8,128)(2,1)S(1)}, bf16[1,256,512]{2,1,0:T(8,128)(2,1)}, u32[]{:S(2)}, u32[]{:S(2)}) collective-permute-start(bf16[1,256,512]{2,1,0:T(8,128)(2,1)S(1)} %all_gather.7), channel_id=1, source_target_pairs={{0,4},{4,8},{8,12},{12,16},{16,20},{20,24},{24,28},{1,5},{5,9},{9,... | collective-permute-start | bytes 786440 | tf_op jit(solution)/shard_map/ppermute | solution.py:16
  28.8 17.6 %collective-permute-start.3 = (bf16[1,256,512]{2,1,0:T(8,128)(2,1)S(1)}, bf16[1,256,512]{2,1,0:T(8,128)(2,1)}, u32[]{:S(2)}, u32[]{:S(2)}) collective-permute-start(bf16[1,256,512]{2,1,0:T(8,128)(2,1)S(1)} %all_gather.7), channel_id=1, source_target_pairs={{4,0},{8,4},{12,8},{16,12},{20,16},{24,20},{28,24},{5,1},{9,5},{13... | collective-permute-start | bytes 786440 | tf_op jit(solution)/shard_map/ppermute | solution.py:17
  33.3 6.1 %copy-start.15 = (bf16[1,1,3,256,256]{4,3,2,1,0:T(8,128)(2,1)}, bf16[1,1,3,256,256]{4,3,2,1,0:T(8,128)(2,1)S(1)}, u32[]{:S(2)}) copy-start(bf16[1,1,3,256,256]{4,3,2,1,0:T(8,128)(2,1)S(1)} %get-tuple-element.17) | copy-start | bytes 1179652
  33.3 6.1 %copy-start.17 = (bf16[1,1,3,256,256]{4,3,2,1,0:T(8,128)(2,1)}, bf16[1,1,3,256,256]{4,3,2,1,0:T(8,128)(2,1)S(1)}, u32[]{:S(2)}) copy-start(bf16[1,1,3,256,256]{4,3,2,1,0:T(8,128)(2,1)S(1)} %get-tuple-element.18) | copy-start | bytes 1179652
  33.3 6.1 %copy-start.13 = (bf16[1,1,3,256,256]{4,3,2,1,0:T(8,128)(2,1)}, bf16[1,1,3,256,256]{4,3,2,1,0:T(8,128)(2,1)S(1)}, u32[]{:S(2)}) copy-start(bf16[1,1,3,256,256]{4,3,2,1,0:T(8,128)(2,1)S(1)} %get-tuple-element.16) | copy-start | bytes 1179652
  33.3 7.0 %copy-start.11 = (bf16[1,1,3,256,256]{4,3,2,1,0:T(8,128)(2,1)}, bf16[1,1,3,256,256]{4,3,2,1,0:T(8,128)(2,1)S(1)}, u32[]{:S(2)}) copy-start(bf16[1,1,3,256,256]{4,3,2,1,0:T(8,128)(2,1)S(1)} %get-tuple-element.15) | copy-start | bytes 1179652
  33.3 7.9 %copy-start.9 = (bf16[1,1,3,256,256]{4,3,2,1,0:T(8,128)(2,1)}, bf16[1,1,3,256,256]{4,3,2,1,0:T(8,128)(2,1)S(1)}, u32[]{:S(2)}) copy-start(bf16[1,1,3,256,256]{4,3,2,1,0:T(8,128)(2,1)S(1)} %get-tuple-element.14) | copy-start | bytes 1179652
  33.3 8.8 %copy-start.7 = (bf16[1,1,3,256,256]{4,3,2,1,0:T(8,128)(2,1)}, bf16[1,1,3,256,256]{4,3,2,1,0:T(8,128)(2,1)S(1)}, u32[]{:S(2)}) copy-start(bf16[1,1,3,256,256]{4,3,2,1,0:T(8,128)(2,1)S(1)} %get-tuple-element.13) | copy-start | bytes 1179652
  33.3 9.8 %copy-start.5 = (bf16[1,1,3,256,256]{4,3,2,1,0:T(8,128)(2,1)}, bf16[1,1,3,256,256]{4,3,2,1,0:T(8,128)(2,1)S(1)}, u32[]{:S(2)}) copy-start(bf16[1,1,3,256,256]{4,3,2,1,0:T(8,128)(2,1)S(1)} %get-tuple-element.12) | copy-start | bytes 1179652
  46.3 21.7 %copy-start.21 = (bf16[1,256,512]{2,1,0:T(8,128)(2,1)}, bf16[1,256,512]{2,1,0:T(8,128)(2,1)S(1)}, u32[]{:S(2)}) copy-start(bf16[1,256,512]{2,1,0:T(8,128)(2,1)S(1)} %get-tuple-element.60) | copy-start | bytes 786436
  49.8 2.8 copy-start.35
  52.6 15.5 %copy-start.23 = (bf16[1,256,512]{2,1,0:T(8,128)(2,1)}, bf16[1,256,512]{2,1,0:T(8,128)(2,1)S(1)}, u32[]{:S(2)}) copy-start(bf16[1,256,512]{2,1,0:T(8,128)(2,1)S(1)} %get-tuple-element.45) | copy-start | bytes 786436
  52.6 15.5 %copy-start.25 = (bf16[1,256,512]{2,1,0:T(8,128)(2,1)}, bf16[1,256,512]{2,1,0:T(8,128)(2,1)S(1)}, u32[]{:S(2)}) copy-start(bf16[1,256,512]{2,1,0:T(8,128)(2,1)S(1)} %get-tuple-element.80) | copy-start | bytes 786436
  69.9 34.4 %reduce-scatter.5.cloned.1.call-start = ((), (), s32[]{:S(2)}) async-start(), calls=%async_computation.3 | async-start | bytes 786432 | tf_op jit(solution)/shard_map/reduce_scatter | solution.py:70
  70.1 1.7 copy-start.19
  70.1 1.7 copy-start.46
  84.1 251.7 %all-reduce.4.cloned.1.call-start = ((), (), s32[]{:S(2)}) async-start(), calls=%async_computation.4 | async-start | bytes 14155776 | tf_op jit(solution)/shard_map/psum | solution.py:74
  85.4 2.6 copy-start.2
  86.7 2.6 copy-start.1
  88.0 2.6 copy-start.4
  89.3 2.6 copy-start.3
  (43 other events, 48.9 us)
Sparse Core Ops, SparseCore 0:
  70.0 9.3 reduce-scatter.2
  84.2 16.0 reduce-scatter.4
Sparse Core Ops, SparseCore 1:
  102.6 233.1 all-reduce.3
where the time goes:
time: 351 us; the launch traced here: 350 us
  waiting for transfers between devices  230 us (66%)
  local copies, waits for them, and re-layouts  33.5 us (10%)
  other arithmetic  26.6 us (8%)
  matrix products  21.7 us (6%)
  between operations  16 us (5%)
  starting transfers between devices  12.7 us (4%)
  blocking collectives  9.65 us (3%)
    psum x1, waiting for transfers between devices, body(): total = lax.psum(local_grad, 'space')  230 us
    unnamed x131, local copies, waits for them, and re-layouts  22.2 us
    dot_general x9, matrix products, body(): jnp.einsum('zfp,zkp->fk', grad_full, window, preferred_element_type=jnp.f...  11.5 us
    mul x5, other arithmetic, plane_window(): return widened[:, :, begin:begin + plane] * masks[col_step]  11.1 us
    ppermute x2, starting transfers between devices, padded(): before = lax.ppermute(last, axis, up)  9.8 us
    reshape x1, local copies, waits for them, and re-layouts, body(): local_grad = jnp.stack(taps).reshape(3, 3, 3, filt_local, chan_local)  8.09 us
    all_gather x1, blocking collectives, body(): panels = lax.all_gather(activation, 'filt', axis=1, tiled=True)  7.36 us
  transfers between devices with their start and end apart: 7, of which 1 were waited for; matrix products, arithmetic and copies ran while one was open for 13% of the time, Pallas kernels for 0%

commit v1 on v0

--- a/solution.py
+++ b/solution.py
@@ -71,7 +71,9 @@
         jnp.bfloat16
     )
     local_grad = jnp.stack(taps).reshape(3, 3, 3, filt_local, chan_local)
-    total = lax.psum(local_grad, "space")
+    total = local_grad
+    for hop in (1, 2, 4):
+        total = total + lax.ppermute(total, "space", [(dev, dev ^ hop) for dev in range(8)])
     cells = depth * lax.axis_size("space") * plane
     kernel_grad = total / jnp.sqrt(jnp.float32(cells))
     return (output, input_grad, kernel_grad)

time: 351 us -> 708 us (2.02)
  waiting for transfers between devices: 230 us -> 580 us
  matrix products: 21.7 us -> 13.9 us
    ppermute x0 -> x3, waiting for transfers between devices: none -> 557 us  [body(): lax.ppermute(total, 'space', [(dev, dev ^ hop) for dev in range(8)])]
    psum x1 -> x0, waiting for transfers between devices: 230 us -> none  [body(): total = lax.psum(local_grad, 'space')]
    add x0 -> x2, other arithmetic: none -> 13.1 us  [body(): total + lax.ppermute(total, 'space', [(dev, dev ^ hop) for dev in range(8)])]
    reduce_scatter x1, waiting for transfers between devices: 0.01 us -> 12.1 us  [body(): lax.psum_scatter(backward, 'filt', scatter_dimension=1, tiled=True)]
    ppermute x2, waiting for transfers between devices: 0.01 us -> 10.7 us  [padded(): before = lax.ppermute(last, axis, up)]
    dot_general x9, matrix products: 11.5 us -> 3.57 us  [body(): jnp.einsum('zfp,zkp->fk', grad_full, window, preferred_element_type=jnp.f...]
    unnamed x131 -> x175, local copies, waits for them, and re-layouts: 22.2 us -> 28.5 us
  transfers between devices with their start and end apart: 7 -> 9, of which waited for: 1 -> 6; matrix products, arithmetic and copies ran while one was open for 13% -> 4% of each run, Pallas kernels for 0% -> 0%
where the time goes in v1:
time: 708 us; the launch traced here: 707 us
  waiting for transfers between devices  580 us (82%)
  local copies, waits for them, and re-layouts  37.8 us (5%)
  other arithmetic  32.4 us (5%)
  starting transfers between devices  18.6 us (3%)
  between operations  14.9 us (2%)
  matrix products  13.9 us (2%)
  blocking collectives  9.66 us (1%)
    ppermute x3, waiting for transfers between devices, body(): lax.ppermute(total, 'space', [(dev, dev ^ hop) for dev in range(8)])  557 us
    unnamed x175, local copies, waits for them, and re-layouts  28.5 us
  transfers between devices with their start and end apart: 9, of which 6 were waited for; matrix products, arithmetic and copies ran while one was open for 4% of the time, Pallas kernels for 0%

profile of v1, /device:TPU:0, one launch (start us, length us, event | category | flops | bytes accessed | tf_op | source)
XLA Modules:
  0.0 707.5 jit_solution(4448855264208471827)
XLA Ops:
  7.2 7.4 %all_gather.6 = bf16[1,256,512]{2,1,0:T(8,128)(2,1)S(1)} all-gather(bf16[1,128,512]{2,1,0:T(8,128)(2,1)} %param.3), channel_id=1, replica_groups=mesh['space'=8,'chan'=2,'filt'=2] {'filt'}, dimensions={1}, use_global_device_ids=true | all-gather | bytes 393216 | tf_op jit(solution)/shard_map/all_gather | solution.py:30
  15.9 4.6 collective-permute-start
  20.4 2.3 all_gather.7
  22.7 4.5 collective-permute-start.2
  27.3 1.3 collective-permute-start.3
  30.8 9.8 %collective-permute-done.2 = bf16[1,256,512]{2,1,0:T(8,128)(2,1)S(1)} collective-permute-done((bf16[1,256,512]{2,1,0:T(8,128)(2,1)S(1)}, bf16[1,256,512]{2,1,0:T(8,128)(2,1)S(1)}, u32[]{:S(2)}, u32[]{:S(2)}) %collective-permute-start.2) | collective-permute-done | bytes 262176 | tf_op jit(solution)/shard_map/ppermute | solution.py:16
  41.2 1.7 slice_multiply_fusion.26
  43.0 3.0 slice_multiply_fusion.2
  52.2 3.0 copy-done
  55.2 8.1 %copy.42 = f32[3,3,3,256,256]{4,3,2,1,0:T(8,128)} copy(f32[3,3,3,256,256]{3,4,2,1,0:T(8,128)} %bitcast.227) | data formatting | bytes 14155776 | tf_op jit(solution)/shard_map/reshape | solution.py:73
  63.3 2.5 collective-permute-start.4
  65.7 152.9 %collective-permute-done.4 = f32[3,3,3,256,256]{4,3,2,1,0:T(8,128)} collective-permute-done((f32[3,3,3,256,256]{4,3,2,1,0:T(8,128)}, f32[3,3,3,256,256]{4,3,2,1,0:T(8,128)}, u32[]{:S(2)}, u32[]{:S(2)}) %collective-permute-start.4) | collective-permute-done | bytes 7077920 | tf_op jit(solution)/shard_map/ppermute | solution.py:76
  218.6 6.0 add.255
  224.7 1.6 collective-permute-start.5
  226.3 152.3 %collective-permute-done.5 = f32[3,3,3,256,256]{4,3,2,1,0:T(8,128)} collective-permute-done((f32[3,3,3,256,256]{4,3,2,1,0:T(8,128)S(1)}, f32[3,3,3,256,256]{4,3,2,1,0:T(8,128)}, u32[]{:S(2)}, u32[]{:S(2)}) %collective-permute-start.5) | collective-permute-done | bytes 7077920 | tf_op jit(solution)/shard_map/ppermute | solution.py:76
  378.6 7.1 add.256
  385.7 2.6 collective-permute-start.6
  389.4 1.9 copy.45
  391.4 1.9 copy.46
  393.3 1.9 copy.47
  400.8 1.7 fusion.58
  425.5 12.1 %reduce-scatter.5.cloned.1.call-done = f32[1,128,512]{1,2,0:T(8,128)} async-done(((f32[1,256,512]{1,2,0:T(8,128)}), f32[1,128,512]{1,2,0:T(8,128)}) %reduce-scatter.5.cloned.1.call-update) | async-done | bytes 262160 | tf_op jit(solution)/shard_map/reduce_scatter | solution.py:70
  439.3 252.1 %collective-permute-done.6 = f32[3,3,3,256,256]{4,3,2,1,0:T(8,128)} collective-permute-done((f32[3,3,3,256,256]{4,3,2,1,0:T(8,128)}, f32[3,3,3,256,256]{4,3,2,1,0:T(8,128)}, u32[]{:S(2)}, u32[]{:S(2)}) %collective-permute-start.6) | collective-permute-done | bytes 7077920 | tf_op jit(solution)/shard_map/ppermute | solution.py:76
  691.4 9.2 %add_multiply_fusion = f32[3,3,3,256,256]{4,3,2,1,0:T(8,128)} fusion(f32[3,3,3,256,256]{4,3,2,1,0:T(8,128)} %add.256, f32[3,3,3,256,256]{4,3,2,1,0:T(8,128)} %collective-permute-done.6), kind=kLoop, calls=%fused_computation | loop fusion | flops 3538944 | bytes 21233664 | tf_op jit(solution)/shard_map/div | solution.py:78
  (222 shorter events, 41.0 us)
Async XLA Ops:
  7.2 416.5 %reduce-scatter.3.cloned.1.call-start = ((), (), s32[]{:S(2)}) async-start(), calls=%async_computation.2 | async-start | bytes 786432 | tf_op jit(solution)/shard_map/reduce_scatter | solution.py:69
  14.6 14.0 %collective-permute-start.1 = (bf16[1,256,512]{2,1,0:T(8,128)(2,1)S(1)}, bf16[1,256,512]{2,1,0:T(8,128)(2,1)S(1)}, u32[]{:S(2)}, u32[]{:S(2)}) collective-permute-start(bf16[1,256,512]{2,1,0:T(8,128)(2,1)S(1)} %all_gather.6), channel_id=1, source_target_pairs={{4,0},{8,4},{12,8},{16,12},{20,16},{24,20},{28,24},{5,1},{9,5},{13... | collective-permute-start | bytes 786440 | tf_op jit(solution)/shard_map/ppermute | solution.py:17
  15.9 13.6 %collective-permute-start = (bf16[1,256,512]{2,1,0:T(8,128)(2,1)S(1)}, bf16[1,256,512]{2,1,0:T(8,128)(2,1)S(1)}, u32[]{:S(2)}, u32[]{:S(2)}) collective-permute-start(bf16[1,256,512]{2,1,0:T(8,128)(2,1)S(1)} %all_gather.6), channel_id=1, source_target_pairs={{0,4},{4,8},{8,12},{12,16},{16,20},{20,24},{24,28},{1,5},{5,9},{9,... | collective-permute-start | bytes 786440 | tf_op jit(solution)/shard_map/ppermute | solution.py:16
  22.7 17.9 %collective-permute-start.2 = (bf16[1,256,512]{2,1,0:T(8,128)(2,1)S(1)}, bf16[1,256,512]{2,1,0:T(8,128)(2,1)S(1)}, u32[]{:S(2)}, u32[]{:S(2)}) collective-permute-start(bf16[1,256,512]{2,1,0:T(8,128)(2,1)S(1)} %all_gather.7), channel_id=1, source_target_pairs={{0,4},{4,8},{8,12},{12,16},{16,20},{20,24},{24,28},{1,5},{5,9},{9,... | collective-permute-start | bytes 786440 | tf_op jit(solution)/shard_map/ppermute | solution.py:16
  27.3 13.4 %collective-permute-start.3 = (bf16[1,256,512]{2,1,0:T(8,128)(2,1)S(1)}, bf16[1,256,512]{2,1,0:T(8,128)(2,1)S(1)}, u32[]{:S(2)}, u32[]{:S(2)}) collective-permute-start(bf16[1,256,512]{2,1,0:T(8,128)(2,1)S(1)} %all_gather.7), channel_id=1, source_target_pairs={{4,0},{8,4},{12,8},{16,12},{20,16},{24,20},{28,24},{5,1},{9,5},{13... | collective-permute-start | bytes 786440 | tf_op jit(solution)/shard_map/ppermute | solution.py:17
  30.7 15.3 %copy-start.27 = (bf16[1,256,512]{2,1,0:T(8,128)(2,1)}, bf16[1,256,512]{2,1,0:T(8,128)(2,1)S(1)}, u32[]{:S(2)}) copy-start(bf16[1,256,512]{2,1,0:T(8,128)(2,1)S(1)} %get-tuple-element.67) | copy-start | bytes 786436
  30.7 15.3 %copy-start.31 = (bf16[1,256,512]{2,1,0:T(8,128)(2,1)}, bf16[1,256,512]{2,1,0:T(8,128)(2,1)S(1)}, u32[]{:S(2)}) copy-start(bf16[1,256,512]{2,1,0:T(8,128)(2,1)S(1)} %get-tuple-element.68) | copy-start | bytes 786436
  30.7 16.8 %copy-start.13 = (bf16[1,256,512]{2,1,0:T(8,128)(2,1)}, bf16[1,256,512]{2,1,0:T(8,128)(2,1)S(1)}, u32[]{:S(2)}) copy-start(bf16[1,256,512]{2,1,0:T(8,128)(2,1)S(1)} %get-tuple-element.65) | copy-start | bytes 786436
  30.7 16.8 %copy-start.21 = (bf16[1,256,512]{2,1,0:T(8,128)(2,1)}, bf16[1,256,512]{2,1,0:T(8,128)(2,1)S(1)}, u32[]{:S(2)}) copy-start(bf16[1,256,512]{2,1,0:T(8,128)(2,1)S(1)} %get-tuple-element.66) | copy-start | bytes 786436
  30.7 17.8 %copy-start.9 = (bf16[1,256,512]{2,1,0:T(8,128)(2,1)}, bf16[1,256,512]{2,1,0:T(8,128)(2,1)S(1)}, u32[]{:S(2)}) copy-start(bf16[1,256,512]{2,1,0:T(8,128)(2,1)S(1)} %get-tuple-element.63) | copy-start | bytes 786436
  30.7 17.8 %copy-start.11 = (bf16[1,256,512]{2,1,0:T(8,128)(2,1)}, bf16[1,256,512]{2,1,0:T(8,128)(2,1)S(1)}, u32[]{:S(2)}) copy-start(bf16[1,256,512]{2,1,0:T(8,128)(2,1)S(1)} %get-tuple-element.64) | copy-start | bytes 786436
  30.8 19.5 %copy-start.5 = (bf16[1,256,512]{2,1,0:T(8,128)(2,1)}, bf16[1,256,512]{2,1,0:T(8,128)(2,1)S(1)}, u32[]{:S(2)}) copy-start(bf16[1,256,512]{2,1,0:T(8,128)(2,1)S(1)} %get-tuple-element.61) | copy-start | bytes 786436
  30.8 19.4 %copy-start.7 = (bf16[1,256,512]{2,1,0:T(8,128)(2,1)}, bf16[1,256,512]{2,1,0:T(8,128)(2,1)S(1)}, u32[]{:S(2)}) copy-start(bf16[1,256,512]{2,1,0:T(8,128)(2,1)S(1)} %get-tuple-element.62) | copy-start | bytes 786436
  30.8 20.9 %copy-start.50 = (bf16[1,256,512]{2,1,0:T(8,128)(2,1)}, bf16[1,256,512]{2,1,0:T(8,128)(2,1)S(1)}, u32[]{:S(2)}) copy-start(bf16[1,256,512]{2,1,0:T(8,128)(2,1)S(1)} %get-tuple-element.60) | copy-start | bytes 786436
  43.0 7.3 %copy-start.15 = (bf16[1,256,512]{2,1,0:T(8,128)(2,1)}, bf16[1,256,512]{2,1,0:T(8,128)(2,1)S(1)}, u32[]{:S(2)}) copy-start(bf16[1,256,512]{2,1,0:T(8,128)(2,1)S(1)} %get-tuple-element.46) | copy-start | bytes 786436
  43.0 7.3 %copy-start.17 = (bf16[1,256,512]{2,1,0:T(8,128)(2,1)}, bf16[1,256,512]{2,1,0:T(8,128)(2,1)S(1)}, u32[]{:S(2)}) copy-start(bf16[1,256,512]{2,1,0:T(8,128)(2,1)S(1)} %get-tuple-element.47) | copy-start | bytes 786436
  43.0 7.3 %copy-start.19 = (bf16[1,256,512]{2,1,0:T(8,128)(2,1)}, bf16[1,256,512]{2,1,0:T(8,128)(2,1)S(1)}, u32[]{:S(2)}) copy-start(bf16[1,256,512]{2,1,0:T(8,128)(2,1)S(1)} %get-tuple-element.79) | copy-start | bytes 786436
  43.0 8.7 %copy-start.52 = (bf16[1,256,512]{2,1,0:T(8,128)(2,1)}, bf16[1,256,512]{2,1,0:T(8,128)(2,1)S(1)}, u32[]{:S(2)}) copy-start(bf16[1,256,512]{2,1,0:T(8,128)(2,1)S(1)} %get-tuple-element.45) | copy-start | bytes 786436
  43.0 8.7 %copy-start.54 = (bf16[1,256,512]{2,1,0:T(8,128)(2,1)}, bf16[1,256,512]{2,1,0:T(8,128)(2,1)S(1)}, u32[]{:S(2)}) copy-start(bf16[1,256,512]{2,1,0:T(8,128)(2,1)S(1)} %get-tuple-element.80) | copy-start | bytes 786436
  63.3 155.3 %collective-permute-start.4 = (f32[3,3,3,256,256]{4,3,2,1,0:T(8,128)}, f32[3,3,3,256,256]{4,3,2,1,0:T(8,128)}, u32[]{:S(2)}, u32[]{:S(2)}) collective-permute-start(f32[3,3,3,256,256]{4,3,2,1,0:T(8,128)} %copy.42), channel_id=1, source_target_pairs={{0,4},{4,0},{8,12},{12,8},{16,20},{20,16},{24,28},{28,24},{1,5},{5... | collective-permute-start | bytes 21233672 | tf_op jit(solution)/shard_map/ppermute | solution.py:76
  224.7 154.0 %collective-permute-start.5 = (f32[3,3,3,256,256]{4,3,2,1,0:T(8,128)S(1)}, f32[3,3,3,256,256]{4,3,2,1,0:T(8,128)}, u32[]{:S(2)}, u32[]{:S(2)}) collective-permute-start(f32[3,3,3,256,256]{4,3,2,1,0:T(8,128)S(1)} %add.255), channel_id=1, source_target_pairs={{0,8},{4,12},{8,0},{12,4},{16,24},{20,28},{24,16},{28,20},{1,9},{5... | collective-permute-start | bytes 21233672 | tf_op jit(solution)/shard_map/ppermute | solution.py:76
  378.6 9.6 %copy-start.1 = (bf16[3,3,3,256,256]{4,3,2,1,0:T(8,128)(2,1)S(1)}, bf16[3,3,3,256,256]{4,3,2,1,0:T(8,128)(2,1)}, u32[]{:S(2)}) copy-start(bf16[3,3,3,256,256]{4,3,2,1,0:T(8,128)(2,1)} %param.4) | copy-start | bytes 10616836
  385.7 305.8 %collective-permute-start.6 = (f32[3,3,3,256,256]{4,3,2,1,0:T(8,128)}, f32[3,3,3,256,256]{4,3,2,1,0:T(8,128)}, u32[]{:S(2)}, u32[]{:S(2)}) collective-permute-start(f32[3,3,3,256,256]{4,3,2,1,0:T(8,128)} %add.256), channel_id=1, source_target_pairs={{0,16},{4,20},{8,24},{12,28},{16,0},{20,4},{24,8},{28,12},{1,17},{... | collective-permute-start | bytes 21233672 | tf_op jit(solution)/shard_map/ppermute | solution.py:76
  412.5 25.0 %reduce-scatter.5.cloned.1.call-start = ((), (), s32[]{:S(2)}) async-start(), calls=%async_computation.3 | async-start | bytes 786432 | tf_op jit(solution)/shard_map/reduce_scatter | solution.py:70
  (67 other events, 110.3 us)
Sparse Core Ops, SparseCore 0:
  412.6 6.7 reduce-scatter.2
  423.8 13.6 reduce-scatter.4
